TPU v7x, 256 devices: a whole 4x4x8 slice. The times are simulated.
256 devices in a mesh: pipe: 8 (over z), seq: 16 (over x, y), tp: 2 (over core).
Axes of the slice: x: 4, y: 4, z: 8, core: 2. Of those that a mesh axis runs over, the one named last changes fastest.
Arguments:
- layer_inputs: bfloat16 [8, 2048, 4096], P('pipe', ('seq', 'tp')), may hold values from -6 to 6
- out_grad: bfloat16 [2048, 4096], P('seq', 'tp'), may hold values from -6 to 6
- short_weights: bfloat16 [8, 7, 3, 4096], P('pipe', None, None, 'tp'), may hold values from -2 to 2
- long_filters: bfloat16 [8, 256, 128], P('pipe', 'tp'), may hold values from -0.15625 to 0.15625
- out_weights: bfloat16 [8, 4096, 4096], P('pipe', 'tp', 'seq'), may hold values from -0.09375 to 0.09375
Outputs:
- input_grad: bfloat16 [8, 2048, 4096], P('pipe', 'seq', 'tp')
- short_grad: float32 [8, 7, 3, 4096], P('pipe', None, None, 'tp')
- long_grad: float32 [8, 256, 128], P('pipe', 'tp')
All inputs are finite; a program needn't handle non-finite values.
Results may differ from a plain program's by a relative error of at most 0.03.
Values may be sent and summed in bfloat16 or wider, within the bound.
No kernel may reach another device: no remote copies, remote signals or barrier semaphores. Data moves between devices by JAX's collectives and lax.ppermute only.
A program may use at most 192 MiB of HBM per device.

v0:
```python
import jax
import jax.numpy as jnp
from jax import lax
from jax.sharding import PartitionSpec as P


def passed_along(array, axis, by):
    size = lax.axis_size(axis)
    pairs = [(i, i + by) for i in range(size) if 0 <= i + by < size]
    return lax.ppermute(array, axis, pairs)


def toeplitz_blocks(filters):
    groups, kernel_width = filters.shape
    base_row = jnp.concatenate(
        [
            jnp.zeros((groups, 1), filters.dtype),
            filters[:, ::-1],
            jnp.zeros((groups, kernel_width), filters.dtype),
        ],
        axis=1,
    )
    tiled = jnp.tile(base_row, (1, kernel_width))[:, : 2 * kernel_width * kernel_width]
    return tiled.reshape(groups, kernel_width, 2 * kernel_width)


def lag_sums(products):
    groups, kernel_width, window = products.shape
    flattened = products.reshape(groups, kernel_width * window)
    flattened = jnp.pad(flattened, ((0, 0), (0, kernel_width)))
    skewed = flattened.reshape(groups, kernel_width, window + 1)
    totals = jnp.sum(skewed, axis=1)
    return totals[:, 1 : kernel_width + 1][:, ::-1]


def to_groups(rows, groups):
    count = rows.shape[0]
    return jnp.transpose(rows.reshape(count, groups, rows.shape[1] // groups), (1, 2, 0))


def from_groups(blocks):
    groups, width, count = blocks.shape
    return jnp.transpose(blocks, (2, 0, 1)).reshape(count, groups * width)


def featurize(source, weights):
    tap_count = weights.shape[0]
    row_count = source.shape[0] - tap_count + 1
    running = jnp.zeros((weights.shape[1], row_count, source.shape[1]), jnp.float32)
    for offset in range(tap_count):
        start = tap_count - 1 - offset
        running = running + weights[offset][:, None, :] * source[start : start + row_count][None]
    return running


def spread_back(feature_grads, weights):
    tap_count = weights.shape[0]
    row_count = feature_grads.shape[1] - tap_count + 1
    running = jnp.zeros((row_count, feature_grads.shape[2]), jnp.float32)
    for offset in range(tap_count):
        running = running + jnp.sum(
            weights[offset][:, None, :] * feature_grads[:, offset : offset + row_count], axis=0
        )
    return running


def weight_grads(feature_grads, source):
    row_count = feature_grads.shape[1]
    tap_count = source.shape[0] - row_count + 1
    terms = []
    for offset in range(tap_count):
        start = tap_count - 1 - offset
        terms.append(jnp.sum(feature_grads * source[start : start + row_count][None], axis=1))
    return jnp.stack(terms)


def long_forward(padded, toeplitz, groups):
    grouped = to_groups(padded, groups)
    result = jnp.einsum("gis,gcs->gci", toeplitz, grouped, preferred_element_type=jnp.float32)
    return from_groups(result)


def long_backward(trailing, reversed_band, groups):
    grouped = to_groups(trailing, groups)
    result = jnp.einsum("grj,gcr->gcj", reversed_band, grouped, preferred_element_type=jnp.float32)
    return from_groups(result)


def filter_grads(mixed_grad, padded, groups):
    grad_groups = to_groups(mixed_grad, groups)
    value_groups = to_groups(padded, groups)
    products = jnp.einsum(
        "gci,gcs->gis", grad_groups, value_groups, preferred_element_type=jnp.float32
    )
    return lag_sums(products)


def recompute(layer_block, weights, filters):
    local_rows = lax.all_to_all(layer_block, "tp", split_axis=1, concat_axis=0, tiled=True)
    tap_count = weights.shape[0]
    kernel_width = filters.shape[1]
    before = passed_along(local_rows[local_rows.shape[0] - tap_count + 1 :], "seq", 1)
    extended = jnp.concatenate([before, local_rows], axis=0).astype(jnp.float32)
    features = featurize(extended, weights)
    products = (features[1] * features[2]).astype(jnp.bfloat16)
    earlier_products = passed_along(products[products.shape[0] - kernel_width + 1 :], "seq", 1)
    padded = jnp.concatenate(
        [jnp.zeros((1, products.shape[1]), jnp.bfloat16), earlier_products, products], axis=0
    )
    toeplitz = toeplitz_blocks(filters)
    reversed_band = jnp.concatenate(
        [toeplitz[:, :, kernel_width:], toeplitz[:, :, :kernel_width]], axis=1
    )
    mixed_rows = long_forward(padded, toeplitz, filters.shape[0])
    return (features, padded, reversed_band, mixed_rows, extended)


def dense_grad(incoming, columns, active):
    empty_sum = jnp.zeros((incoming.shape[0], columns.shape[0]), jnp.float32)
    piece = lax.all_gather(incoming, "tp", axis=1, tiled=True)
    summed = lax.cond(
        active,
        lambda: jnp.einsum("td,cd->tc", piece, columns, preferred_element_type=jnp.float32),
        lambda: empty_sum,
    )
    return summed.astype(jnp.bfloat16)


def backward(saved_state, incoming, dense_part, weights, groups, active):
    features, padded, reversed_band, mixed_rows, source = saved_state
    tap_count = weights.shape[0]
    kernel_width = reversed_band.shape[2]
    token_count, channels = incoming.shape
    edge_rows = tap_count - 1
    dense_float = dense_part.astype(jnp.float32)
    mixed_grad = (dense_float * features[0]).astype(jnp.bfloat16)
    after_grad = passed_along(mixed_grad[: kernel_width - 1], "seq", -1)
    trailing_grad = jnp.concatenate(
        [mixed_grad, after_grad, jnp.zeros((1, channels), jnp.bfloat16)], axis=0
    )

    def middle(operand):
        product_grad = long_backward(operand, reversed_band, groups)
        query_grad = dense_float * mixed_rows
        return (
            jnp.stack([query_grad, product_grad * features[2], product_grad * features[1]]),
            product_grad,
        )

    def middle_skipped(operand):
        return (
            jnp.zeros((3, token_count, channels), jnp.float32),
            jnp.zeros((token_count, channels), jnp.float32),
        )

    feature_grads, product_grad = lax.cond(active, middle, middle_skipped, trailing_grad)
    head_zeros = jnp.zeros((3, edge_rows, channels), jnp.float32)
    partial_sums = spread_back(
        jnp.concatenate([head_zeros, feature_grads[:, :edge_rows]], axis=1), weights
    )
    overflow = passed_along(partial_sums.astype(jnp.bfloat16), "seq", -1).astype(partial_sums.dtype)

    def finish(operands):
        grads, spill = operands
        trailing = jnp.concatenate([grads, head_zeros], axis=1)
        tail_rows = jnp.concatenate(
            [jnp.zeros((token_count - edge_rows, channels), jnp.float32), spill], axis=0
        )
        total = incoming.astype(jnp.float32) + spread_back(trailing, weights) + tail_rows
        return total.astype(jnp.bfloat16)

    def finish_skipped(operands):
        return jnp.zeros((token_count, channels), jnp.bfloat16)

    return (lax.cond(active, finish, finish_skipped, (feature_grads, overflow)), product_grad)


def per_device(layer_inputs, out_grad, short_weights, long_filters, out_weights):
    sections = lax.axis_size("pipe")
    section_index = lax.axis_index("pipe")
    weights = short_weights[0].astype(jnp.float32)
    filters = long_filters[0]
    groups = filters.shape[0]
    saved_state = recompute(layer_inputs[0], weights, filters)
    features, padded, reversed_band, mixed_rows, source = saved_state
    columns = lax.all_gather(out_weights[0], "seq", axis=1, tiled=True)
    incoming = out_grad
    input_result = jnp.zeros_like(out_grad)
    dense_kept = jnp.zeros(out_grad.shape, jnp.bfloat16)
    product_kept = jnp.zeros(out_grad.shape, jnp.float32)
    for step_index in range(sections):
        active = section_index == sections - 1 - step_index
        dense_part = dense_grad(incoming, columns, active)
        input_grad, product_grad = backward(
            saved_state, incoming, dense_part, weights, groups, active
        )
        input_result = jnp.where(active, input_grad, input_result)
        dense_kept = jnp.where(active, dense_part, dense_kept)
        product_kept = jnp.where(active, product_grad, product_kept)
        if step_index + 1 < sections:
            incoming = passed_along(input_grad, "pipe", -1)
    dense_float = dense_kept.astype(jnp.float32)
    mixed_grad = (dense_float * features[0]).astype(jnp.bfloat16)
    feature_grads = jnp.stack(
        [dense_float * mixed_rows, product_kept * features[2], product_kept * features[1]]
    )
    short_local = weight_grads(feature_grads, source)
    long_local = filter_grads(mixed_grad, padded, groups)
    short_result, long_result = (
        lax.psum(short_local.astype(jnp.bfloat16), "seq").astype(jnp.float32),
        lax.psum(long_local.astype(jnp.bfloat16), "seq").astype(jnp.float32),
    )
    return (input_result[None], short_result[None], long_result[None])


def solution(mesh):
    in_specs = (
        P("pipe", ("seq", "tp"), None),
        P("seq", "tp"),
        P("pipe", None, None, "tp"),
        P("pipe", "tp", None),
        P("pipe", "tp", "seq"),
    )
    out_specs = (P("pipe", "seq", "tp"), P("pipe", None, None, "tp"), P("pipe", "tp", None))
    return jax.shard_map(
        per_device, mesh=mesh, in_specs=in_specs, out_specs=out_specs, check_vma=False
    )
```

profile of v0, /device:TPU:2, one launch (start us, length us, event | category | flops | bytes accessed | tf_op | source)
XLA Modules:
  0.0 1388.4 jit_solution(17497464794075836733)
XLA Ops:
  22.8 13.0 tile.10
  42.9 12.6 copy.273
  88.5 68.1 %all-gather.27.cloned.1.call-done = bf16[1,2048,4096]{2,1,0:T(8,128)(2,1)} async-done(((bf16[1,2048,256]{2,1,0:T(8,128)(2,1)}), bf16[1,2048,4096]{2,1,0:T(8,128)(2,1)}) %all-gather.27.cloned.1.call-update) | async-done | bytes 16777232 | tf_op jit(solution)/shard_map/all_gather | solution.py:186
  226.1 11.6 collective-permute-done.4
  237.8 54.5 %all-gather.13.cloned.1.call-done = bf16[128,4096]{1,0:T(8,128)(2,1)} async-done(((bf16[128,2048]{1,0:T(8,128)(2,1)}), bf16[128,4096]{1,0:T(8,128)(2,1)}) %all-gather.13.cloned.1.call-update) | async-done | bytes 1048592 | tf_op jit(solution)/shard_map/all_gather | solution.py:120
  301.8 11.6 collective-permute-done.5
  350.4 13.3 collective-permute-done.7
  363.8 61.0 %all-gather.15.cloned.1.call-done = bf16[128,4096]{1,0:T(8,128)(2,1)} async-done(((bf16[128,2048]{1,0:T(8,128)(2,1)}), bf16[128,4096]{1,0:T(8,128)(2,1)}) %all-gather.15.cloned.1.call-update) | async-done | bytes 1048592 | tf_op jit(solution)/shard_map/all_gather | solution.py:120
  433.8 11.6 collective-permute-done.8
  482.4 13.3 collective-permute-done.10
  495.8 61.7 %all-gather.17.cloned.1.call-done = bf16[128,4096]{1,0:T(8,128)(2,1)} async-done(((bf16[128,2048]{1,0:T(8,128)(2,1)}), bf16[128,4096]{1,0:T(8,128)(2,1)}) %all-gather.17.cloned.1.call-update) | async-done | bytes 1048592 | tf_op jit(solution)/shard_map/all_gather | solution.py:120
  566.6 11.6 collective-permute-done.11
  615.4 13.3 collective-permute-done.13
  628.8 62.6 %all-gather.19.cloned.1.call-done = bf16[128,4096]{1,0:T(8,128)(2,1)} async-done(((bf16[128,2048]{1,0:T(8,128)(2,1)}), bf16[128,4096]{1,0:T(8,128)(2,1)}) %all-gather.19.cloned.1.call-update) | async-done | bytes 1048592 | tf_op jit(solution)/shard_map/all_gather | solution.py:120
  700.6 11.6 collective-permute-done.14
  735.0 10.8 collective-permute-done.15
  749.2 13.3 collective-permute-done.16
  762.6 61.6 %all-gather.21.cloned.1.call-done = bf16[128,4096]{1,0:T(8,128)(2,1)} async-done(((bf16[128,2048]{1,0:T(8,128)(2,1)}), bf16[128,4096]{1,0:T(8,128)(2,1)}) %all-gather.21.cloned.1.call-update) | async-done | bytes 1048592 | tf_op jit(solution)/shard_map/all_gather | solution.py:120
  833.3 11.6 collective-permute-done.17
  882.1 13.3 collective-permute-done.19
  895.5 59.4 %all-gather.23.cloned.1.call-done = bf16[128,4096]{1,0:T(8,128)(2,1)} async-done(((bf16[128,2048]{1,0:T(8,128)(2,1)}), bf16[128,4096]{1,0:T(8,128)(2,1)}) %all-gather.23.cloned.1.call-update) | async-done | bytes 1048592 | tf_op jit(solution)/shard_map/all_gather | solution.py:120
  963.9 11.6 collective-permute-done.20
  1012.5 58.4 %collective-permute-done.22 = bf16[128,2048]{1,0:T(8,128)(2,1)} collective-permute-done((bf16[128,2048]{1,0:T(8,128)(2,1)}, bf16[128,2048]{1,0:T(8,128)(2,1)}, u32[]{:S(2)}, u32[]{:S(2)}) %collective-permute-start.22) | collective-permute-done | bytes 524320 | tf_op jit(solution)/shard_map/ppermute | solution.py:10
  1085.3 17.4 %conditional.45 = (f32[128,2048]{1,0:T(8,128)}, f32[128,2048]{0,1:T(8,128)}, bf16[128,2048]{0,1:T(8,128)(2,1)}) conditional(s32[]{:T(128)} %convert_element_type.282, () %tuple.260, (bf16[128,4096]{1,0:T(8,128)(2,1)}, bf16[2048,4096]{1,0:T(8,128)(2,1)}) %tuple.638), branch_computations={%region_134.135_spmd, %region_135.136_spmd} | conditional | flops 2148007936 | bytes 22020120 | solution.py:121
  1085.5 12.9 fusion.10
  1120.1 17.8 %copy.274 = f32[128,128,256]{0,2,1:T(8,128)} copy(f32[128,128,256]{2,1,0:T(8,128)} %fusion.30) | data formatting | bytes 33554432 | tf_op jit(solution)/shard_map/reshape | solution.py:29
  1137.9 13.3 pad.28
  1151.2 17.5 %reshape.203 = f32[128,128,257]{0,2,1:T(8,128)} reshape(f32[128,32896]{0,1:T(8,128)} %pad.28) | data formatting | bytes 33685504 | tf_op jit(solution)/shard_map/reshape | solution.py:31
  1178.8 64.3 %psum.15 = bf16[1,128,128]{1,2,0:T(8,128)(2,1)} all-reduce(bf16[1,128,128]{1,2,0:T(8,128)(2,1)} %bitcast.399), channel_id=1, replica_groups=mesh['pipe'=8,'seq'=16,'tp'=2] {'seq'}, use_global_device_ids=true, to_apply=%region_162.163 | all-reduce | flops 16384 | bytes 65536 | tf_op jit(solution)/shard_map/psum | solution.py:211
  1248.7 15.2 %conditional.46 = (f32[3,128,2048]{1,2,0:T(8,128)}, f32[128,2048]{0,1:T(8,128)}) conditional(s32[]{:T(128)} %convert_element_type.282, () %tuple.259, (f32[128,2048]{1,0:T(8,128)}, f32[128,2048]{0,1:T(8,128)}, bf16[256,2048]{0,1:T(8,128)(2,1)S(1)}, bf16[128,256,128]{2,1,0:T(8,128)(2,1)}, f32[3,128,2048]{1,2,0:T(8,128)S(1)}) %tuple.646), branch_computations={%region_136.137_spmd, %region_137.138_spmd} | conditional | flops 136577024 | bytes 35651656 | solution.py:156
  1297.2 11.5 conditional.47
  1310.9 68.5 %all-reduce.27.cloned.1.call-done = bf16[1,7,3,2048]{3,1,2,0:T(8,128)(2,1)} async-done(((bf16[1,7,3,2048]{3,1,2,0:T(8,128)(2,1)}), bf16[1,7,3,2048]{3,1,2,0:T(8,128)(2,1)}) %all-reduce.27.cloned.1.call-update) | async-done | bytes 86032 | tf_op jit(solution)/shard_map/psum | solution.py:210
  (302 shorter events, 547.8 us)
Async XLA Ops:
  7.2 81.4 %all-gather.11.cloned.1.call-start = ((), (), s32[]{:S(2)}) async-start(), calls=%async_computation.1 | async-start | bytes 1572864 | tf_op jit(solution)/shard_map/all_gather | solution.py:120
  7.9 148.7 %all-gather.27.cloned.1.call-start = ((), (), s32[]{:S(2)}) async-start(), calls=%async_computation.10 | async-start | bytes 17825792 | tf_op jit(solution)/shard_map/all_gather | solution.py:186
  8.7 283.6 %all-gather.13.cloned.1.call-start = ((), (), s32[]{:S(2)}) async-start(), calls=%async_computation.2 | async-start | bytes 1572864 | tf_op jit(solution)/shard_map/all_gather | solution.py:120
  14.5 48.0 %collective-permute-start = (bf16[6,2048]{1,0:T(8,128)(2,1)S(1)}, bf16[6,2048]{1,0:T(8,128)(2,1)S(1)}, u32[]{:S(2)}, u32[]{:S(2)}) collective-permute-start(bf16[6,2048]{1,0:T(8,128)(2,1)S(1)} %slice.757), channel_id=1, source_target_pairs={{0,2},{2,4},{4,6},{6,8},{8,10},{10,12},{12,14},{14,16},{16,18},{18... | collective-permute-start | bytes 73736 | tf_op jit(solution)/shard_map/ppermute | solution.py:10
  163.9 17.1 %collective-permute-start.1 = (bf16[127,2048]{0,1:T(8,128)(2,1)}, bf16[127,2048]{0,1:T(8,128)(2,1)}, u32[]{:S(2)}, u32[]{:S(2)}) collective-permute-start(bf16[127,2048]{0,1:T(8,128)(2,1)} %slice.773), channel_id=1, source_target_pairs={{0,2},{2,4},{4,6},{6,8},{8,10},{10,12},{12,14},{14,16},{16,18},{18... | collective-permute-start | bytes 1560584 | tf_op jit(solution)/shard_map/ppermute | solution.py:10
  166.0 16.1 %collective-permute-start.2 = (bf16[127,2048]{0,1:T(8,128)(2,1)}, bf16[127,2048]{0,1:T(8,128)(2,1)}, u32[]{:S(2)}, u32[]{:S(2)}) collective-permute-start(bf16[127,2048]{0,1:T(8,128)(2,1)} %bitcast.344), channel_id=1, source_target_pairs={{2,0},{4,2},{6,4},{8,6},{10,8},{12,10},{14,12},{16,14},{18,16},{20... | collective-permute-start | bytes 1560584 | tf_op jit(solution)/shard_map/ppermute | solution.py:10
  207.3 15.6 %collective-permute-start.3 = (bf16[6,2048]{0,1:T(8,128)(2,1)S(1)}, bf16[6,2048]{0,1:T(8,128)(2,1)S(1)}, u32[]{:S(2)}, u32[]{:S(2)}) collective-permute-start(bf16[6,2048]{0,1:T(8,128)(2,1)S(1)} %add_convert_fusion.15), channel_id=1, source_target_pairs={{2,0},{4,2},{6,4},{8,6},{10,8},{12,10},{14,12},{16,14},{18,16},{20... | collective-permute-start | bytes 73736 | tf_op jit(solution)/shard_map/ppermute | solution.py:10
  237.7 187.0 %all-gather.15.cloned.1.call-start = ((), (), s32[]{:S(2)}) async-start(), calls=%async_computation.3 | async-start | bytes 1572864 | tf_op jit(solution)/shard_map/all_gather | solution.py:120
  297.1 16.3 %collective-permute-start.5 = (bf16[127,2048]{0,1:T(8,128)(2,1)S(1)}, bf16[127,2048]{0,1:T(8,128)(2,1)S(1)}, u32[]{:S(2)}, u32[]{:S(2)}) collective-permute-start(bf16[127,2048]{0,1:T(8,128)(2,1)S(1)} %bitcast.392), channel_id=1, source_target_pairs={{2,0},{4,2},{6,4},{8,6},{10,8},{12,10},{14,12},{16,14},{18,16},{20... | collective-permute-start | bytes 1560584 | tf_op jit(solution)/shard_map/ppermute | solution.py:10
  329.6 17.3 %collective-permute-start.6 = (bf16[6,2048]{0,1:T(8,128)(2,1)S(1)}, bf16[6,2048]{0,1:T(8,128)(2,1)S(1)}, u32[]{:S(2)}, u32[]{:S(2)}) collective-permute-start(bf16[6,2048]{0,1:T(8,128)(2,1)S(1)} %add_convert_fusion.14), channel_id=1, source_target_pairs={{2,0},{4,2},{6,4},{8,6},{10,8},{12,10},{14,12},{16,14},{18,16},{20... | collective-permute-start | bytes 73736 | tf_op jit(solution)/shard_map/ppermute | solution.py:10
  349.1 14.6 %collective-permute-start.7 = (bf16[128,2048]{1,0:T(8,128)(2,1)}, bf16[128,2048]{1,0:T(8,128)(2,1)}, u32[]{:S(2)}, u32[]{:S(2)}) collective-permute-start(bf16[128,2048]{1,0:T(8,128)(2,1)} %get-tuple-element.1088), channel_id=1, source_target_pairs={{32,0},{64,32},{96,64},{128,96},{160,128},{192,160},{224,192},{33,... | collective-permute-start | bytes 1572872 | tf_op jit(solution)/shard_map/ppermute | solution.py:10
  363.7 193.8 %all-gather.17.cloned.1.call-start = ((), (), s32[]{:S(2)}) async-start(), calls=%async_computation.4 | async-start | bytes 1572864 | tf_op jit(solution)/shard_map/all_gather | solution.py:120
  429.1 16.3 %collective-permute-start.8 = (bf16[127,2048]{0,1:T(8,128)(2,1)S(1)}, bf16[127,2048]{0,1:T(8,128)(2,1)S(1)}, u32[]{:S(2)}, u32[]{:S(2)}) collective-permute-start(bf16[127,2048]{0,1:T(8,128)(2,1)S(1)} %bitcast.393), channel_id=1, source_target_pairs={{2,0},{4,2},{6,4},{8,6},{10,8},{12,10},{14,12},{16,14},{18,16},{20... | collective-permute-start | bytes 1560584 | tf_op jit(solution)/shard_map/ppermute | solution.py:10
  461.9 17.3 %collective-permute-start.9 = (bf16[6,2048]{0,1:T(8,128)(2,1)S(1)}, bf16[6,2048]{0,1:T(8,128)(2,1)S(1)}, u32[]{:S(2)}, u32[]{:S(2)}) collective-permute-start(bf16[6,2048]{0,1:T(8,128)(2,1)S(1)} %add_convert_fusion.13), channel_id=1, source_target_pairs={{2,0},{4,2},{6,4},{8,6},{10,8},{12,10},{14,12},{16,14},{18,16},{20... | collective-permute-start | bytes 73736 | tf_op jit(solution)/shard_map/ppermute | solution.py:10
  481.1 14.6 %collective-permute-start.10 = (bf16[128,2048]{1,0:T(8,128)(2,1)}, bf16[128,2048]{1,0:T(8,128)(2,1)}, u32[]{:S(2)}, u32[]{:S(2)}) collective-permute-start(bf16[128,2048]{1,0:T(8,128)(2,1)} %get-tuple-element.1089), channel_id=1, source_target_pairs={{32,0},{64,32},{96,64},{128,96},{160,128},{192,160},{224,192},{33,... | collective-permute-start | bytes 1572872 | tf_op jit(solution)/shard_map/ppermute | solution.py:10
  495.7 195.7 %all-gather.19.cloned.1.call-start = ((), (), s32[]{:S(2)}) async-start(), calls=%async_computation.5 | async-start | bytes 1572864 | tf_op jit(solution)/shard_map/all_gather | solution.py:120
  562.0 16.3 %collective-permute-start.11 = (bf16[127,2048]{0,1:T(8,128)(2,1)S(1)}, bf16[127,2048]{0,1:T(8,128)(2,1)S(1)}, u32[]{:S(2)}, u32[]{:S(2)}) collective-permute-start(bf16[127,2048]{0,1:T(8,128)(2,1)S(1)} %bitcast.394), channel_id=1, source_target_pairs={{2,0},{4,2},{6,4},{8,6},{10,8},{12,10},{14,12},{16,14},{18,16},{20... | collective-permute-start | bytes 1560584 | tf_op jit(solution)/shard_map/ppermute | solution.py:10
  594.9 17.3 %collective-permute-start.12 = (bf16[6,2048]{0,1:T(8,128)(2,1)S(1)}, bf16[6,2048]{0,1:T(8,128)(2,1)S(1)}, u32[]{:S(2)}, u32[]{:S(2)}) collective-permute-start(bf16[6,2048]{0,1:T(8,128)(2,1)S(1)} %add_convert_fusion.12), channel_id=1, source_target_pairs={{2,0},{4,2},{6,4},{8,6},{10,8},{12,10},{14,12},{16,14},{18,16},{20... | collective-permute-start | bytes 73736 | tf_op jit(solution)/shard_map/ppermute | solution.py:10
  614.1 14.6 %collective-permute-start.13 = (bf16[128,2048]{1,0:T(8,128)(2,1)}, bf16[128,2048]{1,0:T(8,128)(2,1)}, u32[]{:S(2)}, u32[]{:S(2)}) collective-permute-start(bf16[128,2048]{1,0:T(8,128)(2,1)} %get-tuple-element.1090), channel_id=1, source_target_pairs={{32,0},{64,32},{96,64},{128,96},{160,128},{192,160},{224,192},{33,... | collective-permute-start | bytes 1572872 | tf_op jit(solution)/shard_map/ppermute | solution.py:10
  628.8 195.5 %all-gather.21.cloned.1.call-start = ((), (), s32[]{:S(2)}) async-start(), calls=%async_computation.6 | async-start | bytes 1572864 | tf_op jit(solution)/shard_map/all_gather | solution.py:120
  696.0 16.3 %collective-permute-start.14 = (bf16[127,2048]{0,1:T(8,128)(2,1)S(1)}, bf16[127,2048]{0,1:T(8,128)(2,1)S(1)}, u32[]{:S(2)}, u32[]{:S(2)}) collective-permute-start(bf16[127,2048]{0,1:T(8,128)(2,1)S(1)} %bitcast.395), channel_id=1, source_target_pairs={{2,0},{4,2},{6,4},{8,6},{10,8},{12,10},{14,12},{16,14},{18,16},{20... | collective-permute-start | bytes 1560584 | tf_op jit(solution)/shard_map/ppermute | solution.py:10
  728.5 17.3 %collective-permute-start.15 = (bf16[6,2048]{0,1:T(8,128)(2,1)S(1)}, bf16[6,2048]{0,1:T(8,128)(2,1)S(1)}, u32[]{:S(2)}, u32[]{:S(2)}) collective-permute-start(bf16[6,2048]{0,1:T(8,128)(2,1)S(1)} %add_convert_fusion.11), channel_id=1, source_target_pairs={{2,0},{4,2},{6,4},{8,6},{10,8},{12,10},{14,12},{16,14},{18,16},{20... | collective-permute-start | bytes 73736 | tf_op jit(solution)/shard_map/ppermute | solution.py:10
  747.9 14.6 %collective-permute-start.16 = (bf16[128,2048]{1,0:T(8,128)(2,1)}, bf16[128,2048]{1,0:T(8,128)(2,1)}, u32[]{:S(2)}, u32[]{:S(2)}) collective-permute-start(bf16[128,2048]{1,0:T(8,128)(2,1)} %get-tuple-element.1091), channel_id=1, source_target_pairs={{32,0},{64,32},{96,64},{128,96},{160,128},{192,160},{224,192},{33,... | collective-permute-start | bytes 1572872 | tf_op jit(solution)/shard_map/ppermute | solution.py:10
  762.6 192.3 %all-gather.23.cloned.1.call-start = ((), (), s32[]{:S(2)}) async-start(), calls=%async_computation.7 | async-start | bytes 1572864 | tf_op jit(solution)/shard_map/all_gather | solution.py:120
  828.7 16.3 %collective-permute-start.17 = (bf16[127,2048]{0,1:T(8,128)(2,1)S(1)}, bf16[127,2048]{0,1:T(8,128)(2,1)S(1)}, u32[]{:S(2)}, u32[]{:S(2)}) collective-permute-start(bf16[127,2048]{0,1:T(8,128)(2,1)S(1)} %bitcast.396), channel_id=1, source_target_pairs={{2,0},{4,2},{6,4},{8,6},{10,8},{12,10},{14,12},{16,14},{18,16},{20... | collective-permute-start | bytes 1560584 | tf_op jit(solution)/shard_map/ppermute | solution.py:10
  861.6 17.3 %collective-permute-start.18 = (bf16[6,2048]{0,1:T(8,128)(2,1)S(1)}, bf16[6,2048]{0,1:T(8,128)(2,1)S(1)}, u32[]{:S(2)}, u32[]{:S(2)}) collective-permute-start(bf16[6,2048]{0,1:T(8,128)(2,1)S(1)} %add_convert_fusion.10), channel_id=1, source_target_pairs={{2,0},{4,2},{6,4},{8,6},{10,8},{12,10},{14,12},{16,14},{18,16},{20... | collective-permute-start | bytes 73736 | tf_op jit(solution)/shard_map/ppermute | solution.py:10
  895.4 189.9 %all-gather.25.cloned.1.call-start = ((), (), s32[]{:S(2)}) async-start(), calls=%async_computation.8 | async-start | bytes 1572864 | tf_op jit(solution)/shard_map/all_gather | solution.py:120
  959.3 16.3 %collective-permute-start.20 = (bf16[127,2048]{0,1:T(8,128)(2,1)S(1)}, bf16[127,2048]{0,1:T(8,128)(2,1)S(1)}, u32[]{:S(2)}, u32[]{:S(2)}) collective-permute-start(bf16[127,2048]{0,1:T(8,128)(2,1)S(1)} %bitcast.397), channel_id=1, source_target_pairs={{2,0},{4,2},{6,4},{8,6},{10,8},{12,10},{14,12},{16,14},{18,16},{20... | collective-permute-start | bytes 1560584 | tf_op jit(solution)/shard_map/ppermute | solution.py:10
  992.0 17.3 %collective-permute-start.21 = (bf16[6,2048]{0,1:T(8,128)(2,1)S(1)}, bf16[6,2048]{0,1:T(8,128)(2,1)S(1)}, u32[]{:S(2)}, u32[]{:S(2)}) collective-permute-start(bf16[6,2048]{0,1:T(8,128)(2,1)S(1)} %add_convert_fusion.9), channel_id=1, source_target_pairs={{2,0},{4,2},{6,4},{8,6},{10,8},{12,10},{14,12},{16,14},{18,16},{20... | collective-permute-start | bytes 73736 | tf_op jit(solution)/shard_map/ppermute | solution.py:10
  1011.2 59.7 %collective-permute-start.22 = (bf16[128,2048]{1,0:T(8,128)(2,1)}, bf16[128,2048]{1,0:T(8,128)(2,1)}, u32[]{:S(2)}, u32[]{:S(2)}) collective-permute-start(bf16[128,2048]{1,0:T(8,128)(2,1)} %get-tuple-element.1093), channel_id=1, source_target_pairs={{32,0},{64,32},{96,64},{128,96},{160,128},{192,160},{224,192},{33,... | collective-permute-start | bytes 1572872 | tf_op jit(solution)/shard_map/ppermute | solution.py:10
  1070.9 308.5 %all-reduce.27.cloned.1.call-start = ((), (), s32[]{:S(2)}) async-start(), calls=%async_computation.9 | async-start | bytes 196608 | tf_op jit(solution)/shard_map/psum | solution.py:210
  1105.5 141.5 %collective-permute-start.23 = (bf16[127,2048]{0,1:T(8,128)(2,1)}, bf16[127,2048]{0,1:T(8,128)(2,1)}, u32[]{:S(2)}, u32[]{:S(2)}) collective-permute-start(bf16[127,2048]{0,1:T(8,128)(2,1)} %bitcast.351), channel_id=1, source_target_pairs={{2,0},{4,2},{6,4},{8,6},{10,8},{12,10},{14,12},{16,14},{18,16},{20... | collective-permute-start | bytes 1560584 | tf_op jit(solution)/shard_map/ppermute | solution.py:10
  (34 other events, 160.9 us)
Sparse Core Ops, SparseCore 0:
  9.8 17.3 all-gather.10
  29.6 127.0 all-gather.26
  237.8 54.4 all-gather.12
  363.8 60.8 all-gather.14
  495.8 61.6 all-gather.16
  628.9 62.4 all-gather.18
  762.7 61.4 all-gather.20
  895.6 59.2 all-gather.22
  1071.1 13.2 all-gather.24
  1289.0 90.3 all-reduce.26
where the time goes:
time: 1400 us; the launch traced here: 1390 us
  waiting for transfers between devices  790 us (56%)
  local copies, waits for them, and re-layouts  192 us (14%)
  other arithmetic  183 us (13%)
  starting transfers between devices  103 us (7%)
  blocking collectives  68.4 us (5%)
  matrix products  33.7 us (2%)
  between operations  15.6 us (1%)
    all_gather x8, waiting for transfers between devices, dense_grad(): piece = lax.all_gather(incoming, 'tp', axis=1, tiled=True)  361 us
    ppermute x25, waiting for transfers between devices, passed_along(): return lax.ppermute(array, axis, pairs)  291 us
    ppermute x25, starting transfers between devices, passed_along(): return lax.ppermute(array, axis, pairs)  102 us
    reduce_sum x10, other arithmetic, spread_back(): jnp.sum(weights[offset][:, None, :] * feature_grads[:, offset:offset + ro...  82 us
    psum x1, waiting for transfers between devices, per_device(): lax.psum(short_local.astype(jnp.bfloat16), 'seq').astype(jnp.float32)  68.5 us
    all_gather x1, waiting for transfers between devices, per_device(): columns = lax.all_gather(out_weights[0], 'seq', axis=1, tiled=True)  68.1 us
    psum x1, blocking collectives, per_device(): lax.psum(long_local.astype(jnp.bfloat16), 'seq').astype(jnp.float32)  64.3 us
    another operation x46, local copies, waits for them, and re-layouts  46.8 us
  transfers between devices with their start and end apart: 35, of which 31 were waited for; matrix products, arithmetic and copies ran while one was open for 13% of the time, Pallas kernels for 0%

commit v1 on v0

v1 whole, which is shorter than its diff:
```python
import functools

import jax
import jax.numpy as jnp
from jax import lax
from jax.experimental import pallas as pl
from jax.experimental.pallas import tpu as pltpu
from jax.sharding import PartitionSpec as P

KL = 128
KS = 7
TILE = 128
GW = 16
AUX = 48
EDGE = 8
PAD = 16
WIN = 2 * KL
BF = jnp.bfloat16
F32 = jnp.float32
VMEM_LIMIT = 60 * 1024 * 1024
INTERPRET = False


def call(body, out_shape, *args, **kwargs):
    return pl.pallas_call(
        body,
        out_shape=out_shape,
        compiler_params=pltpu.CompilerParams(vmem_limit_bytes=VMEM_LIMIT),
        interpret=INTERPRET,
        **kwargs,
    )(*args)


def shape(dims, dtype):
    return jax.ShapeDtypeStruct(dims, dtype)


def dot(a, b):
    return jnp.dot(a, b, preferred_element_type=F32)


def dot_nt(a, b):
    return lax.dot_general(a, b, (((1,), (1,)), ((), ())), preferred_element_type=F32)


def swap_matrix(width):
    size = TILE // width
    n = size * TILE
    row = lax.broadcasted_iota(jnp.int32, (n, n), 0)
    col = lax.broadcasted_iota(jnp.int32, (n, n), 1)
    a, b, j = row // TILE, (row // width) % size, row % width
    return (col == b * TILE + a * width + j).astype(F32).astype(BF)


def split_owned(x, planes, width, matrix):
    step = planes * width
    slices = x.shape[1] // step
    size = TILE // width
    pieces = [[None] * (slices // size) for _ in range(planes)]
    for a in range(slices // size):
        for b in range(planes // size):
            tiles = [
                x[:, (a * size + i) * step + b * TILE : (a * size + i) * step + (b + 1) * TILE]
                for i in range(size)
            ]
            moved = dot(jnp.concatenate(tiles, axis=1), matrix).astype(BF)
            for i in range(size):
                pieces[b * size + i][a] = moved[:, i * TILE : (i + 1) * TILE]
    return [jnp.concatenate(p, axis=1) for p in pieces]


def join_owned(parts, width, matrix):
    planes = len(parts)
    size = TILE // width
    slices = parts[0].shape[1] // width
    out = [[None] * (planes // size) for _ in range(slices)]
    for a in range(slices // size):
        for b in range(planes // size):
            tiles = [parts[b * size + i][:, a * TILE : (a + 1) * TILE] for i in range(size)]
            moved = dot(jnp.concatenate(tiles, axis=1), matrix)
            for i in range(size):
                out[a * size + i][b] = moved[:, i * TILE : (i + 1) * TILE]
    return jnp.concatenate([jnp.concatenate(o, axis=1) for o in out], axis=1)


def filter_rows(slices, planes, per):
    n = slices * planes * per
    row = lax.broadcasted_iota(jnp.int32, (n, n), 0)
    col = lax.broadcasted_iota(jnp.int32, (n, n), 1)
    z, k, g = row // (slices * per), (row // per) % slices, row % per
    return (col == k * planes * per + z * per + g).astype(F32).astype(BF)


def pack_body(planes, slices, width, w_ref, sw_ref, lf_ref, out_ref):
    owned = slices * width
    depth = planes * width
    for z in range(planes):
        block = w_ref[:, z].reshape(owned, depth)
        turned = block.astype(F32).T.astype(BF)
        out_ref[:, z * width : (z + 1) * width, :] = turned.reshape(planes, width, owned)
    base = planes * width
    matrix = swap_matrix(width)
    taps = split_owned(sw_ref[...], planes, width, matrix)
    per = width // GW
    mover = filter_rows(slices, planes, per)
    filters = dot(mover, lf_ref[...]).astype(BF)
    count = slices * per
    zeros = jnp.zeros((GW, owned), BF)
    for z in range(planes):
        out_ref[z, base : base + 32, :] = taps[z]
        out_ref[z, base + 32 : base + AUX, :] = zeros
        out_ref[z, base + 32 : base + 32 + count, :KL] = filters[z * count : (z + 1) * count]


def shuffle_body(planes, halves, width, x_ref, out_ref):
    matrix = swap_matrix(width)
    half = x_ref.shape[1] // halves
    for h in range(halves):
        pieces = split_owned(x_ref[:, h * half : (h + 1) * half], planes, width, matrix)
        for z in range(planes):
            out_ref[z * halves + h] = pieces[z]


def grouped(toeplitz, rows_per, source, groups):
    channels = source.shape[1]
    tiles = []
    for u in range(channels // TILE):
        per = TILE // GW
        full = dot(toeplitz[u * per * rows_per : (u + 1) * per * rows_per], source[:, u * TILE : (u + 1) * TILE])
        lane = lax.broadcasted_iota(jnp.int32, (rows_per, TILE), 1) // GW
        merged = full[:rows_per]
        for g in range(1, per):
            merged = jnp.where(lane == g, full[g * rows_per : (g + 1) * rows_per], merged)
        tiles.append(merged)
    return jnp.concatenate(tiles, axis=1)


def edge_rows(ref, groups):
    return jnp.concatenate(
        [ref[g * KL + KL - PAD : (g + 1) * KL, :] for g in range(groups)], axis=0
    )


def recompute_body(
    groups, own_ref, prev_ref, prev2_ref, next_ref, aux_ref,
    f0_ref, f1_ref, f2_ref, mixed_ref, back_ref, turned_ref,
    rows_ref, band_ref,
):
    rows_ref[0:PAD, :] = prev2_ref[...].astype(F32)
    rows_ref[PAD : PAD + KL, :] = prev_ref[...].astype(F32)
    rows_ref[PAD + KL : PAD + 2 * KL, :] = own_ref[...].astype(F32)
    rows_ref[PAD + 2 * KL :, :] = next_ref[...].astype(F32)
    taps = aux_ref[0:32, :].astype(F32)

    def feature(f, first, count):
        start = PAD + KL + first
        total = taps[f : f + 1] * rows_ref[start : start + count, :]
        for j in range(1, KS):
            total = total + taps[3 * j + f : 3 * j + f + 1] * rows_ref[start - j : start - j + count, :]
        return total

    f0_ref[...] = feature(0, 0, KL)
    key_tail = feature(1, 0, KL + EDGE)
    value_tail = feature(2, 0, KL + EDGE)
    f1_ref[...] = key_tail
    f2_ref[...] = value_tail
    kv = jnp.concatenate([feature(1, -KL, KL) * feature(2, -KL, KL), key_tail * value_tail], axis=0)
    window = kv[:WIN].astype(BF)
    late = kv[EDGE : EDGE + WIN].astype(BF)

    filters = aux_ref[32 : 32 + groups, :KL]
    tap = lax.broadcasted_iota(jnp.int32, (KL, WIN), 0)
    lane = lax.broadcasted_iota(jnp.int32, (KL, WIN), 1)
    ahead = dot(filters, (lane == KL - tap).astype(F32).astype(BF))
    behind = dot(filters, (lane == tap).astype(F32).astype(BF))
    for g in range(groups):
        wide = jnp.broadcast_to(ahead[g : g + 1], (KL, WIN))
        band_ref[g * KL : (g + 1) * KL, :] = pltpu.roll(wide, 0, 1, stride=1, stride_axis=0).astype(BF)
        wide = jnp.broadcast_to(behind[g : g + 1], (KL, WIN))
        back_ref[g * KL : (g + 1) * KL, :] = pltpu.roll(wide, 0, 1, stride=1, stride_axis=0).astype(BF)
    mixed_ref[0:KL, :] = grouped(band_ref, KL, window, groups)
    mixed_ref[KL:, :] = grouped(edge_rows(band_ref, groups), PAD, late, groups)[PAD - EDGE :]
    source = lax.broadcasted_iota(jnp.int32, (WIN, WIN), 0)
    target = lax.broadcasted_iota(jnp.int32, (WIN, WIN), 1)
    mirror = (source + target == WIN - 1).astype(F32).astype(BF)
    turned_ref[...] = dot(mirror, window).astype(BF)


def project_body(tp_ref, own_ref, other_ref, w_ref, out_ref):
    first = tp_ref[0] == 0
    own, other = own_ref[...], other_ref[...]
    low = jnp.where(first, own, other)
    high = jnp.where(first, other, own)
    slices, _, width, owned = w_ref.shape
    half = slices // 2
    total = dot(low, w_ref[:half].reshape(half * width, owned))
    total = total + dot(high, w_ref[half:].reshape(half * width, owned))
    out_ref[0] = total.astype(BF)


def gate_body(parts_ref, f0_ref, send_ref, dgate_ref, early_ref):
    total = parts_ref[0].astype(F32)
    for z in range(1, parts_ref.shape[0]):
        total = total + parts_ref[z].astype(F32)
    dgate = total.astype(BF)
    dmixed = (dgate.astype(F32) * f0_ref[...]).astype(BF)
    send_ref[0:KL, :] = dmixed
    send_ref[KL:, :] = dgate[:PAD]
    dgate_ref[...] = dgate
    early_ref[...] = dmixed[:PAD]


def finish_body(
    groups, send_ref, dgate_ref, near_ref, far_ref, f1_ref, f2_ref, mixed_ref, back_ref, aux_ref, grad_ref,
    out_ref, dkv_ref, d0_ref, d1_ref, d2_ref,
):
    rows = jnp.concatenate(
        [send_ref[0:KL, :], near_ref[0:KL, :], far_ref[...]], axis=0
    )
    window = rows[:WIN]
    late = rows.astype(F32)[EDGE : EDGE + WIN].astype(BF)
    main = grouped(back_ref, KL, window, groups)
    tail = grouped(edge_rows(back_ref, groups), PAD, late, groups)[PAD - EDGE :]
    dkv_ref[...] = main
    d0_ref[0:KL, :] = dgate_ref[...].astype(F32) * mixed_ref[0:KL, :]
    d0_ref[KL:, :] = near_ref[KL:, :].astype(F32)[:EDGE] * mixed_ref[KL:, :]
    d1_ref[0:KL, :] = main * f2_ref[0:KL, :]
    d1_ref[KL:, :] = tail * f2_ref[KL:, :]
    d2_ref[0:KL, :] = main * f1_ref[0:KL, :]
    d2_ref[KL:, :] = tail * f1_ref[KL:, :]
    taps = aux_ref[0:32, :].astype(F32)
    total = grad_ref[...].astype(F32)
    for j in range(KS):
        for f, ref in enumerate((d0_ref, d1_ref, d2_ref)):
            total = total + taps[3 * j + f : 3 * j + f + 1] * ref[j : j + KL, :]
    out_ref[...] = total.astype(BF)


def filters_body(
    groups, dgate_ref, mixed_ref, dkv_ref, f1_ref, f2_ref, own_ref, prev_ref, send_ref, turned_ref,
    out_ref, rows_ref, skew_ref,
):
    channels = own_ref.shape[1]
    rows_ref[0:PAD, :] = prev_ref[KL - PAD :, :].astype(F32)
    rows_ref[PAD:, :] = own_ref[...].astype(F32)
    dkv = dkv_ref[...]
    grads = (
        dgate_ref[...].astype(F32) * mixed_ref[0:KL, :],
        dkv * f2_ref[0:KL, :],
        dkv * f1_ref[0:KL, :],
    )
    sums = []
    for j in range(KS):
        source = rows_ref[PAD - j : PAD - j + KL, :]
        for f in range(3):
            sums.append(jnp.sum(grads[f] * source, axis=0, keepdims=True))
    sums.append(jnp.zeros((32 - 3 * KS, channels), F32))
    out_ref[0:32, :] = jnp.concatenate(sums, axis=0).astype(BF)
    lags = []
    per = TILE // GW
    lane = lax.broadcasted_iota(jnp.int32, (KL, TILE), 1) // GW
    for u in range(channels // TILE):
        grad = send_ref[0:KL, u * TILE : (u + 1) * TILE].astype(F32)
        stacked = jnp.concatenate(
            [jnp.where(lane == g, grad, 0.0).astype(BF) for g in range(per)], axis=0
        )
        skew_ref[...] = dot_nt(stacked, turned_ref[:, u * TILE : (u + 1) * TILE])
        for g in range(per):
            rolled = pltpu.roll(skew_ref[g * KL : (g + 1) * KL, :], 0, 1, stride=1, stride_axis=0)
            lags.append(jnp.sum(rolled, axis=0, keepdims=True))
    if groups < GW:
        lags.append(jnp.zeros((GW - groups, WIN), F32))
    sums = pltpu.roll(jnp.concatenate(lags, axis=0), WIN - (KL - 1), 1)
    out_ref[32:AUX, :] = jnp.zeros((AUX - 32, channels), BF)
    out_ref[32:AUX, :KL] = sums[:, :KL].astype(BF)


def collect_body(width, in_ref, grad_ref, part_ref):
    planes = in_ref.shape[0]
    matrix = swap_matrix(width)
    joined = join_owned([in_ref[z, 0:KL, :] for z in range(planes)], width, matrix)
    grad_ref[...] = joined.astype(BF)
    halves = in_ref.shape[2] // TILE
    for z in range(planes):
        for u in range(halves):
            part_ref[z * halves + u] = in_ref[z, KL:, u * TILE : (u + 1) * TILE]


def sum_body(copies, in_ref, out_ref):
    total = in_ref[0].astype(F32)
    for s in range(1, in_ref.shape[0]):
        total = total + in_ref[s].astype(F32)
    value = total.astype(BF)
    for s in range(copies):
        out_ref[s] = value


def spread_body(planes, slices, width, in_ref, short_ref, long_ref):
    halves = in_ref.shape[0] // planes
    matrix = swap_matrix(width)
    parts = [
        jnp.concatenate([in_ref[z * halves + u, 0:32, :] for u in range(halves)], axis=1)
        for z in range(planes)
    ]
    short_ref[...] = join_owned(parts, width, matrix)
    per = width // GW
    count = slices * per
    stacked = jnp.concatenate(
        [in_ref[z * halves, 32 : 32 + count, :] for z in range(planes)], axis=0
    )
    mover = filter_rows(slices, planes, per)
    long_ref[...] = lax.dot_general(
        mover, stacked, (((0,), (0,)), ((), ())), preferred_element_type=F32
    )


def from_next(x, by):
    size = lax.axis_size("seq")
    return lax.ppermute(x, "seq", [(i, i - by) for i in range(by, size)])


def from_before(x, by):
    size = lax.axis_size("seq")
    return lax.ppermute(x, "seq", [(i, i + by) for i in range(size - by)])


def per_device(layer_inputs, out_grad, short_weights, long_filters, out_weights):
    planes = lax.axis_size("pipe")
    blocks = lax.axis_size("seq")
    depth = out_weights.shape[2]
    half = out_grad.shape[1]
    width = depth // planes
    slices = half // depth
    owned = slices * width
    groups = owned // GW
    tokens = out_grad.shape[0]
    dims = long_filters.shape[1]

    taps = jnp.pad(short_weights[0].reshape(KS * 3, half), ((0, 32 - KS * 3), (0, 0)))
    packed = call(
        functools.partial(pack_body, planes, slices, width),
        shape((planes, planes * width + AUX, owned), BF),
        out_weights[0].reshape(slices, planes, width, depth),
        taps,
        long_filters[0],
    )
    packed = lax.all_to_all(packed, "pipe", 0, 0, tiled=True)
    base = planes * width
    aux = [packed[p, base:] for p in range(planes)]

    def gathered(p):
        whole = lax.all_gather(packed[p, :base], "seq", axis=0)
        return whole.reshape(blocks, planes, width, owned)

    shuffled = call(
        functools.partial(shuffle_body, planes, 2, width),
        shape((planes * 2, layer_inputs.shape[1], owned), BF),
        layer_inputs[0],
    )
    rows = lax.all_to_all(shuffled, ("pipe", "tp"), 0, 0, tiled=True)
    rows = rows.reshape(planes, tokens, owned)
    before = from_before(rows, 1)
    before2 = from_before(rows[:, tokens - PAD :], 2)
    after = from_next(rows[:, :PAD], 1)

    def recomputed(p):
        return call(
            functools.partial(recompute_body, groups),
            (
                shape((KL, owned), F32),
                shape((KL + EDGE, owned), F32),
                shape((KL + EDGE, owned), F32),
                shape((KL + EDGE, owned), F32),
                shape((groups * KL, WIN), BF),
                shape((WIN, owned), BF),
            ),
            rows[p],
            before[p],
            before2[p],
            after[p],
            aux[p],
            scratch_shapes=[
                pltpu.VMEM((2 * KL + 2 * PAD, owned), F32),
                pltpu.VMEM((groups * KL, WIN), BF),
            ],
        )

    tp_index = lax.axis_index("tp").astype(jnp.int32).reshape(1)
    starts = call(
        functools.partial(shuffle_body, planes, 1, width),
        shape((planes, tokens, owned), BF),
        out_grad,
    )
    grad = lax.dynamic_index_in_dim(starts, lax.axis_index("pipe"), 0, keepdims=False)

    outs = [None] * planes
    for p in range(planes - 1, -1, -1):
        weights = gathered(p)
        f0, f1, f2, mixed, back, turned = recomputed(p)
        other = lax.ppermute(grad, "tp", [(0, 1), (1, 0)])
        partial = pl.pallas_call(
            project_body,
            out_shape=shape((planes, tokens, owned), BF),
            grid_spec=pltpu.PrefetchScalarGridSpec(
                num_scalar_prefetch=1,
                grid=(planes,),
                in_specs=[
                    pl.BlockSpec((tokens, owned), lambda z, t: (0, 0)),
                    pl.BlockSpec((tokens, owned), lambda z, t: (0, 0)),
                    pl.BlockSpec((blocks, 1, width, owned), lambda z, t: (0, z, 0, 0)),
                ],
                out_specs=pl.BlockSpec((1, tokens, owned), lambda z, t: (z, 0, 0)),
            ),
            compiler_params=pltpu.CompilerParams(vmem_limit_bytes=VMEM_LIMIT),
            interpret=INTERPRET,
        )(tp_index, grad, other, weights)
        parts = lax.all_to_all(partial, "pipe", 0, 0, tiled=True)
        send, dgate, early = call(
            gate_body,
            (
                shape((KL + PAD, owned), BF),
                shape((KL, owned), BF),
                shape((PAD, owned), BF),
            ),
            parts,
            f0,
        )
        near = from_next(send, 1)
        far = from_next(early, 2)
        new_grad, dkv = call(
            functools.partial(finish_body, groups),
            (shape((KL, owned), BF), shape((KL, owned), F32)),
            send,
            dgate,
            near,
            far,
            f1,
            f2,
            mixed,
            back,
            aux[p],
            grad,
            scratch_shapes=[pltpu.VMEM((KL + EDGE, owned), F32)] * 3,
        )
        filter_grads = call(
            functools.partial(filters_body, groups),
            shape((AUX, owned), BF),
            dgate,
            mixed,
            dkv,
            f1,
            f2,
            rows[p],
            before[p],
            send,
            turned,
            scratch_shapes=[
                pltpu.VMEM((KL + PAD, owned), F32),
                pltpu.VMEM((TILE // GW * KL, WIN), F32),
            ],
        )
        outs[p] = jnp.concatenate([new_grad, filter_grads], axis=0)
        grad = new_grad

    results = lax.all_to_all(jnp.stack(outs), "pipe", 0, 0, tiled=True)
    chunks = planes * owned // TILE
    input_grad, local_sums = call(
        functools.partial(collect_body, width),
        (shape((tokens, half), BF), shape((chunks, AUX, TILE), BF)),
        results,
    )
    exchanged = lax.all_to_all(local_sums, "seq", 0, 0, tiled=True)
    summed = call(
        functools.partial(sum_body, blocks), shape((blocks, AUX, TILE), BF), exchanged
    )
    totals = lax.all_to_all(summed, "seq", 0, 0, tiled=True)
    short_result, long_result = call(
        functools.partial(spread_body, planes, slices, width),
        (shape((32, half), F32), shape((dims, KL), F32)),
        totals,
    )
    short_result = short_result[: KS * 3].reshape(1, KS, 3, half)
    return input_grad[None], short_result, long_result[None]


def solution(mesh):
    in_specs = (
        P("pipe", ("seq", "tp"), None),
        P("seq", "tp"),
        P("pipe", None, None, "tp"),
        P("pipe", "tp", None),
        P("pipe", "tp", "seq"),
    )
    out_specs = (P("pipe", "seq", "tp"), P("pipe", None, None, "tp"), P("pipe", "tp", None))
    return jax.shard_map(
        per_device, mesh=mesh, in_specs=in_specs, out_specs=out_specs, check_vma=False
    )
```

time: 1400 us -> 612 us (0.44)
  waiting for transfers between devices: 790 us -> 191 us
  other arithmetic: 183 us -> 0.92 us
  local copies, waits for them, and re-layouts: 192 us -> 24.9 us
  Pallas kernels: 0 us -> 153 us
  matrix products: 33.7 us -> 0 us
  starting transfers between devices: 103 us -> 127 us
  blocking collectives: 68.4 us -> 88.8 us
    all_gather x9 -> x8, waiting for transfers between devices: 429 us -> 41.6 us  [gathered(): whole = lax.all_gather(packed[p, :base], 'seq', axis=0)]
    ppermute x25 -> x27, waiting for transfers between devices: 291 us -> 31.9 us  [the longest x17 31.8 us: from_next(): return lax.ppermute(x, 'seq', [(i, i - by) for i in range(by, size)])]
    pallas_call x0 -> x46, Pallas kernels: none -> 153 us  [the longest x38 105 us: call(): pl.pallas_call(body, out_shape=out_shape, compiler_params=pltpu.CompilerP...]
    all_to_all x0 -> x9, waiting for transfers between devices: none -> 114 us  [the longest x8 102 us: per_device(): parts = lax.all_to_all(partial, 'pipe', 0, 0, tiled=True)]
    reduce_sum x12 -> x0, other arithmetic: 95.2 us -> none  [the longest x10 82 us: spread_back(): jnp.sum(weights[offset][:, None, :] * feature_grads[:, offset:offset + ro...]
    all_to_all x1 -> x4, blocking collectives: 4.15 us -> 88.8 us  [the longest x1 41.4 us: per_device(): packed = lax.all_to_all(packed, 'pipe', 0, 0, tiled=True)]
    psum x1 -> x0, waiting for transfers between devices: 68.5 us -> none  [per_device(): lax.psum(short_local.astype(jnp.bfloat16), 'seq').astype(jnp.float32)]
    another operation x50 -> x1, local copies, waits for them, and re-layouts: 64.9 us -> 0.08 us  [per_device(): short_weights[0].reshape(KS * 3, half)]
  transfers between devices with their start and end apart: 35 -> 44, of which waited for: 31 -> 24; matrix products, arithmetic and copies ran while one was open for 13% -> 1% of each run, Pallas kernels for 0% -> 22%
where the time goes in v1:
time: 612 us; the launch traced here: 601 us
  waiting for transfers between devices  191 us (31%)
  Pallas kernels  153 us (25%)
  starting transfers between devices  127 us (21%)
  blocking collectives  88.8 us (15%)
  local copies, waits for them, and re-layouts  24.9 us (4%)
  between operations  15.1 us (2%)
    pallas_call x38, Pallas kernels, call(): pl.pallas_call(body, out_shape=out_shape, compiler_params=pltpu.CompilerP...  105 us
    all_to_all x8, waiting for transfers between devices, per_device(): parts = lax.all_to_all(partial, 'pipe', 0, 0, tiled=True)  102 us
    ppermute x17, starting transfers between devices, from_next(): return lax.ppermute(x, 'seq', [(i, i - by) for i in range(by, size)])  63.1 us
    all_to_all x8, starting transfers between devices, per_device(): parts = lax.all_to_all(partial, 'pipe', 0, 0, tiled=True)  53.4 us
    pallas_call x8, Pallas kernels, per_device(): pl.pallas_call(project_body, out_shape=shape((planes, tokens, owned), BF)...  47.8 us
    all_gather x8, waiting for transfers between devices, gathered(): whole = lax.all_gather(packed[p, :base], 'seq', axis=0)  41.6 us
    all_to_all x1, blocking collectives, per_device(): packed = lax.all_to_all(packed, 'pipe', 0, 0, tiled=True)  41.4 us
    ppermute x17, waiting for transfers between devices, from_next(): return lax.ppermute(x, 'seq', [(i, i - by) for i in range(by, size)])  31.8 us
  transfers between devices with their start and end apart: 44, of which 24 were waited for; matrix products, arithmetic and copies ran while one was open for 1% of the time, Pallas kernels for 22%

profile of v1, /device:TPU:2, one launch (start us, length us, event | category | flops | bytes accessed | tf_op | source)
XLA Modules:
  0.0 600.7 jit_solution(6894413269392422699)
XLA Ops:
  11.9 41.4 %all_to_all.65 = bf16[8,304,256]{2,1,0:T(8,128)(2,1)S(1)} all-to-all(bf16[8,304,256]{2,1,0:T(8,128)(2,1)} %shard_map.77), channel_id=1, replica_groups=mesh['pipe'=8,'seq'=16,'tp'=2] {'pipe'}, dimensions={0} | all-to-all | bytes 2490368 | tf_op jit(solution)/shard_map/all_to_all | solution.py:347
  67.5 12.3 %all-to-all-done.2 = bf16[16,64,256]{2,1,0:T(8,128)(2,1)S(1)} async-done(((bf16[16,64,256]{2,1,0:T(8,128)(2,1)}), bf16[16,64,256]{2,1,0:T(8,128)(2,1)S(1)}, u32[]{:S(2)}, u32[]{:S(2)}) %all-to-all-start.2) | async-done | bytes 524320 | tf_op jit(solution)/shard_map/all_to_all | solution.py:360
  91.6 17.3 %all-gather.9.cloned.1.call-done = bf16[16,256,256]{2,1,0:T(8,128)(2,1)} async-done(((bf16[1,256,256]{2,1,0:T(8,128)(2,1)}), bf16[16,256,256]{2,1,0:T(8,128)(2,1)}) %all-gather.9.cloned.1.call-update) | async-done | bytes 2097168 | tf_op jit(solution)/shard_map/all_gather | solution.py:352
  108.9 6.0 shard_map.78
  125.6 10.8 %all-to-all-done.1.parts_ref = bf16[8,128,256]{2,1,0:T(8,128)(2,1)S(1)} async-done(((bf16[8,128,256]{2,1,0:T(8,128)(2,1)}), bf16[8,128,256]{2,1,0:T(8,128)(2,1)S(1)}, u32[]{:S(2)}, u32[]{:S(2)}) %all-to-all-start.1) | async-done | bytes 524320 | tf_op jit(solution)/shard_map/all_to_all | solution.py:417
  158.8 6.0 shard_map.83
  164.8 7.0 %all-to-all-start.3 = ((bf16[8,128,256]{2,1,0:T(8,128)(2,1)}), bf16[8,128,256]{2,1,0:T(8,128)(2,1)S(1)}, u32[]{:S(2)}, u32[]{:S(2)}) async-start(bf16[8,128,256]{2,1,0:T(8,128)(2,1)} %shard_map.83), calls=%async_computation.3 | async-start | bytes 1048576 | tf_op jit(solution)/shard_map/all_to_all | solution.py:417
  175.3 13.1 %all-to-all-done.3.parts_ref = bf16[8,128,256]{2,1,0:T(8,128)(2,1)S(1)} async-done(((bf16[8,128,256]{2,1,0:T(8,128)(2,1)}), bf16[8,128,256]{2,1,0:T(8,128)(2,1)S(1)}, u32[]{:S(2)}, u32[]{:S(2)}) %all-to-all-start.3) | async-done | bytes 524320 | tf_op jit(solution)/shard_map/all_to_all | solution.py:417
  198.3 4.6 collective-permute-done.8.far_ref
  210.6 6.0 shard_map.87
  216.6 7.2 %all-to-all-start.4 = ((bf16[8,128,256]{2,1,0:T(8,128)(2,1)}), bf16[8,128,256]{2,1,0:T(8,128)(2,1)S(1)}, u32[]{:S(2)}, u32[]{:S(2)}) async-start(bf16[8,128,256]{2,1,0:T(8,128)(2,1)} %shard_map.87), calls=%async_computation.4 | async-start | bytes 1048576 | tf_op jit(solution)/shard_map/all_to_all | solution.py:417
  227.4 13.0 %all-to-all-done.4.parts_ref = bf16[8,128,256]{2,1,0:T(8,128)(2,1)S(1)} async-done(((bf16[8,128,256]{2,1,0:T(8,128)(2,1)}), bf16[8,128,256]{2,1,0:T(8,128)(2,1)S(1)}, u32[]{:S(2)}, u32[]{:S(2)}) %all-to-all-start.4) | async-done | bytes 524320 | tf_op jit(solution)/shard_map/all_to_all | solution.py:417
  250.4 4.6 collective-permute-done.11.far_ref
  262.4 6.0 shard_map.91
  268.4 6.9 %all-to-all-start.5 = ((bf16[8,128,256]{2,1,0:T(8,128)(2,1)}), bf16[8,128,256]{2,1,0:T(8,128)(2,1)S(1)}, u32[]{:S(2)}, u32[]{:S(2)}) async-start(bf16[8,128,256]{2,1,0:T(8,128)(2,1)} %shard_map.91), calls=%async_computation.5 | async-start | bytes 1048576 | tf_op jit(solution)/shard_map/all_to_all | solution.py:417
  279.5 12.4 %all-to-all-done.5.parts_ref = bf16[8,128,256]{2,1,0:T(8,128)(2,1)S(1)} async-done(((bf16[8,128,256]{2,1,0:T(8,128)(2,1)}), bf16[8,128,256]{2,1,0:T(8,128)(2,1)S(1)}, u32[]{:S(2)}, u32[]{:S(2)}) %all-to-all-start.5) | async-done | bytes 524320 | tf_op jit(solution)/shard_map/all_to_all | solution.py:417
  313.9 6.0 shard_map.95
  319.9 7.0 %all-to-all-start.6 = ((bf16[8,128,256]{2,1,0:T(8,128)(2,1)}), bf16[8,128,256]{2,1,0:T(8,128)(2,1)S(1)}, u32[]{:S(2)}, u32[]{:S(2)}) async-start(bf16[8,128,256]{2,1,0:T(8,128)(2,1)} %shard_map.95), calls=%async_computation.6 | async-start | bytes 1048576 | tf_op jit(solution)/shard_map/all_to_all | solution.py:417
  330.5 13.1 %all-to-all-done.6.parts_ref = bf16[8,128,256]{2,1,0:T(8,128)(2,1)S(1)} async-done(((bf16[8,128,256]{2,1,0:T(8,128)(2,1)}), bf16[8,128,256]{2,1,0:T(8,128)(2,1)S(1)}, u32[]{:S(2)}, u32[]{:S(2)}) %all-to-all-start.6) | async-done | bytes 524320 | tf_op jit(solution)/shard_map/all_to_all | solution.py:417
  365.6 6.0 shard_map.99
  371.6 7.0 %all-to-all-start.7 = ((bf16[8,128,256]{2,1,0:T(8,128)(2,1)}), bf16[8,128,256]{2,1,0:T(8,128)(2,1)S(1)}, u32[]{:S(2)}, u32[]{:S(2)}) async-start(bf16[8,128,256]{2,1,0:T(8,128)(2,1)} %shard_map.99), calls=%async_computation.7 | async-start | bytes 1048576 | tf_op jit(solution)/shard_map/all_to_all | solution.py:417
  382.1 13.1 %all-to-all-done.7.parts_ref = bf16[8,128,256]{2,1,0:T(8,128)(2,1)S(1)} async-done(((bf16[8,128,256]{2,1,0:T(8,128)(2,1)}), bf16[8,128,256]{2,1,0:T(8,128)(2,1)S(1)}, u32[]{:S(2)}, u32[]{:S(2)}) %all-to-all-start.7) | async-done | bytes 524320 | tf_op jit(solution)/shard_map/all_to_all | solution.py:417
  417.4 6.0 shard_map.103
  423.4 7.0 %all-to-all-start.8 = ((bf16[8,128,256]{2,1,0:T(8,128)(2,1)}), bf16[8,128,256]{2,1,0:T(8,128)(2,1)S(1)}, u32[]{:S(2)}, u32[]{:S(2)}) async-start(bf16[8,128,256]{2,1,0:T(8,128)(2,1)} %shard_map.103), calls=%async_computation.8 | async-start | bytes 1048576 | tf_op jit(solution)/shard_map/all_to_all | solution.py:417
  434.0 13.1 %all-to-all-done.8.parts_ref = bf16[8,128,256]{2,1,0:T(8,128)(2,1)S(1)} async-done(((bf16[8,128,256]{2,1,0:T(8,128)(2,1)}), bf16[8,128,256]{2,1,0:T(8,128)(2,1)S(1)}, u32[]{:S(2)}, u32[]{:S(2)}) %all-to-all-start.8) | async-done | bytes 524320 | tf_op jit(solution)/shard_map/all_to_all | solution.py:417
  457.0 4.6 collective-permute-done.23.far_ref
  469.3 6.0 shard_map.107
  475.2 7.0 %all-to-all-start.9 = ((bf16[8,128,256]{2,1,0:T(8,128)(2,1)}), bf16[8,128,256]{2,1,0:T(8,128)(2,1)S(1)}, u32[]{:S(2)}, u32[]{:S(2)}) async-start(bf16[8,128,256]{2,1,0:T(8,128)(2,1)} %shard_map.107), calls=%async_computation.9 | async-start | bytes 1048576 | tf_op jit(solution)/shard_map/all_to_all | solution.py:417
  485.8 13.1 %all-to-all-done.9.parts_ref = bf16[8,128,256]{2,1,0:T(8,128)(2,1)S(1)} async-done(((bf16[8,128,256]{2,1,0:T(8,128)(2,1)}), bf16[8,128,256]{2,1,0:T(8,128)(2,1)S(1)}, u32[]{:S(2)}, u32[]{:S(2)}) %all-to-all-start.9) | async-done | bytes 524320 | tf_op jit(solution)/shard_map/all_to_all | solution.py:417
  537.9 22.7 %all_to_all.66.in_ref = bf16[8,176,256]{2,1,0:T(8,128)(2,1)} all-to-all(bf16[8,176,256]{2,1,0:T(8,128)(2,1)S(1)} %fusion.7), channel_id=1, replica_groups=mesh['pipe'=8,'seq'=16,'tp'=2] {'pipe'}, dimensions={0} | all-to-all | bytes 1441792 | tf_op jit(solution)/shard_map/all_to_all | solution.py:465
  563.1 12.4 %all_to_all.67.in_ref = bf16[16,48,128]{2,1,0:T(8,128)(2,1)} all-to-all(bf16[16,48,128]{2,1,0:T(8,128)(2,1)} %get-tuple-element.184), channel_id=1, replica_groups=mesh['pipe'=8,'seq'=16,'tp'=2] {'seq'}, dimensions={0} | all-to-all | bytes 393216 | tf_op jit(solution)/shard_map/all_to_all | solution.py:472
  577.2 12.3 %all_to_all.68.in_ref = bf16[16,48,128]{2,1,0:T(8,128)(2,1)} all-to-all(bf16[16,48,128]{2,1,0:T(8,128)(2,1)} %shard_map.120), channel_id=1, replica_groups=mesh['pipe'=8,'seq'=16,'tp'=2] {'seq'}, dimensions={0} | all-to-all | bytes 393216 | tf_op jit(solution)/shard_map/all_to_all | solution.py:476
  (229 shorter events, 254.7 us)
Async XLA Ops:
  7.2 101.8 %all-gather.9.cloned.1.call-start = ((), (), s32[]{:S(2)}) async-start(), calls=%async_computation.13 | async-start | bytes 2228224 | tf_op jit(solution)/shard_map/all_gather | solution.py:352
  54.3 103.9 %all-gather.11.cloned.1.call-start = ((), (), s32[]{:S(2)}) async-start(), calls=%async_computation.14 | async-start | bytes 2228224 | tf_op jit(solution)/shard_map/all_gather | solution.py:352
  55.0 154.9 %all-gather.13.cloned.1.call-start = ((), (), s32[]{:S(2)}) async-start(), calls=%async_computation.15 | async-start | bytes 2228224 | tf_op jit(solution)/shard_map/all_gather | solution.py:352
  55.8 206.0 %all-gather.15.cloned.1.call-start = ((), (), s32[]{:S(2)}) async-start(), calls=%async_computation.16 | async-start | bytes 2228224 | tf_op jit(solution)/shard_map/all_gather | solution.py:352
  56.4 257.0 %all-gather.17.cloned.1.call-start = ((), (), s32[]{:S(2)}) async-start(), calls=%async_computation.17 | async-start | bytes 2228224 | tf_op jit(solution)/shard_map/all_gather | solution.py:352
  56.9 308.0 %all-gather.19.cloned.1.call-start = ((), (), s32[]{:S(2)}) async-start(), calls=%async_computation.18 | async-start | bytes 2228224 | tf_op jit(solution)/shard_map/all_gather | solution.py:352
  60.3 19.5 %all-to-all-start.2 = ((bf16[16,64,256]{2,1,0:T(8,128)(2,1)}), bf16[16,64,256]{2,1,0:T(8,128)(2,1)S(1)}, u32[]{:S(2)}, u32[]{:S(2)}) async-start(bf16[16,64,256]{2,1,0:T(8,128)(2,1)} %shard_map.79), calls=%async_computation.2 | async-start | bytes 1048576 | tf_op jit(solution)/shard_map/all_to_all | solution.py:360
  63.9 352.9 %all-gather.21.cloned.1.call-start = ((), (), s32[]{:S(2)}) async-start(), calls=%async_computation.19 | async-start | bytes 2228224 | tf_op jit(solution)/shard_map/all_gather | solution.py:352
  67.2 24.4 %collective-permute-start = (bf16[128,256]{1,0:T(8,128)(2,1)S(1)}, bf16[128,256]{1,0:T(8,128)(2,1)S(1)}, u32[]{:S(2)}, u32[]{:S(2)}) collective-permute-start(bf16[128,256]{1,0:T(8,128)(2,1)S(1)} %dynamic-slice_bitcast_fusion.own_ref.grad_ref), channel_id=1, source_target_pairs={{0,1},{1,0},{2,3},{3,2},{4,5},{5,4},{6,7},{7,6},{8,9},{9,8},{10,11... | collective-permute-start | bytes 196616 | tf_op jit(solution)/shard_map/ppermute | solution.py:400
  79.8 40.7 %collective-permute-start.1 = (bf16[8,128,256]{2,1,0:T(8,128)(2,1)S(1)}, bf16[8,128,256]{2,1,0:T(8,128)(2,1)S(1)}, u32[]{:S(2)}, u32[]{:S(2)}) collective-permute-start(bf16[8,128,256]{2,1,0:T(8,128)(2,1)S(1)} %bitcast.121), channel_id=1, source_target_pairs={{0,2},{2,4},{4,6},{6,8},{8,10},{10,12},{12,14},{14,16},{16,18},{18... | collective-permute-start | bytes 1572872 | tf_op jit(solution)/shard_map/ppermute | solution.py:324
  83.3 35.8 %collective-permute-start.3 = (bf16[8,16,256]{2,1,0:T(8,128)(2,1)S(1)}, bf16[8,16,256]{2,1,0:T(8,128)(2,1)S(1)}, u32[]{:S(2)}, u32[]{:S(2)}) collective-permute-start(bf16[8,16,256]{2,1,0:T(8,128)(2,1)S(1)} %get-tuple-element.228), channel_id=1, source_target_pairs={{2,0},{4,2},{6,4},{8,6},{10,8},{12,10},{14,12},{16,14},{18,16},{20... | collective-permute-start | bytes 196616 | tf_op jit(solution)/shard_map/ppermute | solution.py:319
  87.8 32.0 %collective-permute-start.2 = (bf16[8,16,256]{2,1,0:T(8,128)(2,1)S(1)}, bf16[8,16,256]{2,1,0:T(8,128)(2,1)S(1)}, u32[]{:S(2)}, u32[]{:S(2)}) collective-permute-start(bf16[8,16,256]{2,1,0:T(8,128)(2,1)S(1)} %get-tuple-element.229), channel_id=1, source_target_pairs={{0,4},{2,6},{4,8},{6,10},{8,12},{10,14},{12,16},{14,18},{16,20},{1... | collective-permute-start | bytes 196616 | tf_op jit(solution)/shard_map/ppermute | solution.py:324
  114.9 21.4 %all-to-all-start.1 = ((bf16[8,128,256]{2,1,0:T(8,128)(2,1)}), bf16[8,128,256]{2,1,0:T(8,128)(2,1)S(1)}, u32[]{:S(2)}, u32[]{:S(2)}) async-start(bf16[8,128,256]{2,1,0:T(8,128)(2,1)} %shard_map.78), calls=%async_computation.1 | async-start | bytes 1048576 | tf_op jit(solution)/shard_map/all_to_all | solution.py:417
  138.9 11.4 %collective-permute-start.4 = (bf16[144,256]{1,0:T(8,128)(2,1)}, bf16[144,256]{1,0:T(8,128)(2,1)S(1)}, u32[]{:S(2)}, u32[]{:S(2)}) collective-permute-start(bf16[144,256]{1,0:T(8,128)(2,1)} %get-tuple-element.96.send_ref), channel_id=1, source_target_pairs={{2,0},{4,2},{6,4},{8,6},{10,8},{12,10},{14,12},{16,14},{18,16},{20... | collective-permute-start | bytes 221192 | tf_op jit(solution)/shard_map/ppermute | solution.py:319
  164.8 23.7 %all-to-all-start.3 = ((bf16[8,128,256]{2,1,0:T(8,128)(2,1)}), bf16[8,128,256]{2,1,0:T(8,128)(2,1)S(1)}, u32[]{:S(2)}, u32[]{:S(2)}) async-start(bf16[8,128,256]{2,1,0:T(8,128)(2,1)} %shard_map.83), calls=%async_computation.3 | async-start | bytes 1048576 | tf_op jit(solution)/shard_map/all_to_all | solution.py:417
  191.0 12.0 %collective-permute-start.7 = (bf16[144,256]{1,0:T(8,128)(2,1)}, bf16[144,256]{1,0:T(8,128)(2,1)S(1)}, u32[]{:S(2)}, u32[]{:S(2)}) collective-permute-start(bf16[144,256]{1,0:T(8,128)(2,1)} %get-tuple-element.105.send_ref), channel_id=1, source_target_pairs={{2,0},{4,2},{6,4},{8,6},{10,8},{12,10},{14,12},{16,14},{18,16},{20... | collective-permute-start | bytes 221192 | tf_op jit(solution)/shard_map/ppermute | solution.py:319
  195.6 7.4 %collective-permute-start.8 = (bf16[16,256]{1,0:T(8,128)(2,1)}, bf16[16,256]{1,0:T(8,128)(2,1)S(1)}, u32[]{:S(2)}, u32[]{:S(2)}) collective-permute-start(bf16[16,256]{1,0:T(8,128)(2,1)} %get-tuple-element.107), channel_id=1, source_target_pairs={{4,0},{6,2},{8,4},{10,6},{12,8},{14,10},{16,12},{18,14},{20,16},{2... | collective-permute-start | bytes 24584 | tf_op jit(solution)/shard_map/ppermute | solution.py:319
  216.6 23.8 %all-to-all-start.4 = ((bf16[8,128,256]{2,1,0:T(8,128)(2,1)}), bf16[8,128,256]{2,1,0:T(8,128)(2,1)S(1)}, u32[]{:S(2)}, u32[]{:S(2)}) async-start(bf16[8,128,256]{2,1,0:T(8,128)(2,1)} %shard_map.87), calls=%async_computation.4 | async-start | bytes 1048576 | tf_op jit(solution)/shard_map/all_to_all | solution.py:417
  243.0 12.0 %collective-permute-start.10 = (bf16[144,256]{1,0:T(8,128)(2,1)}, bf16[144,256]{1,0:T(8,128)(2,1)S(1)}, u32[]{:S(2)}, u32[]{:S(2)}) collective-permute-start(bf16[144,256]{1,0:T(8,128)(2,1)} %get-tuple-element.114.send_ref), channel_id=1, source_target_pairs={{2,0},{4,2},{6,4},{8,6},{10,8},{12,10},{14,12},{16,14},{18,16},{20... | collective-permute-start | bytes 221192 | tf_op jit(solution)/shard_map/ppermute | solution.py:319
  247.6 7.4 %collective-permute-start.11 = (bf16[16,256]{1,0:T(8,128)(2,1)}, bf16[16,256]{1,0:T(8,128)(2,1)S(1)}, u32[]{:S(2)}, u32[]{:S(2)}) collective-permute-start(bf16[16,256]{1,0:T(8,128)(2,1)} %get-tuple-element.116), channel_id=1, source_target_pairs={{4,0},{6,2},{8,4},{10,6},{12,8},{14,10},{16,12},{18,14},{20,16},{2... | collective-permute-start | bytes 24584 | tf_op jit(solution)/shard_map/ppermute | solution.py:319
  268.4 23.5 %all-to-all-start.5 = ((bf16[8,128,256]{2,1,0:T(8,128)(2,1)}), bf16[8,128,256]{2,1,0:T(8,128)(2,1)S(1)}, u32[]{:S(2)}, u32[]{:S(2)}) async-start(bf16[8,128,256]{2,1,0:T(8,128)(2,1)} %shard_map.91), calls=%async_computation.5 | async-start | bytes 1048576 | tf_op jit(solution)/shard_map/all_to_all | solution.py:417
  275.3 193.4 %all-gather.23.cloned.1.call-start = ((), (), s32[]{:S(2)}) async-start(), calls=%async_computation.20 | async-start | bytes 2228224 | tf_op jit(solution)/shard_map/all_gather | solution.py:352
  294.5 12.0 %collective-permute-start.13 = (bf16[144,256]{1,0:T(8,128)(2,1)}, bf16[144,256]{1,0:T(8,128)(2,1)S(1)}, u32[]{:S(2)}, u32[]{:S(2)}) collective-permute-start(bf16[144,256]{1,0:T(8,128)(2,1)} %get-tuple-element.123.send_ref), channel_id=1, source_target_pairs={{2,0},{4,2},{6,4},{8,6},{10,8},{12,10},{14,12},{16,14},{18,16},{20... | collective-permute-start | bytes 221192 | tf_op jit(solution)/shard_map/ppermute | solution.py:319
  319.9 23.7 %all-to-all-start.6 = ((bf16[8,128,256]{2,1,0:T(8,128)(2,1)}), bf16[8,128,256]{2,1,0:T(8,128)(2,1)S(1)}, u32[]{:S(2)}, u32[]{:S(2)}) async-start(bf16[8,128,256]{2,1,0:T(8,128)(2,1)} %shard_map.95), calls=%async_computation.6 | async-start | bytes 1048576 | tf_op jit(solution)/shard_map/all_to_all | solution.py:417
  346.2 11.9 %collective-permute-start.16 = (bf16[144,256]{1,0:T(8,128)(2,1)}, bf16[144,256]{1,0:T(8,128)(2,1)S(1)}, u32[]{:S(2)}, u32[]{:S(2)}) collective-permute-start(bf16[144,256]{1,0:T(8,128)(2,1)} %get-tuple-element.132.send_ref), channel_id=1, source_target_pairs={{2,0},{4,2},{6,4},{8,6},{10,8},{12,10},{14,12},{16,14},{18,16},{20... | collective-permute-start | bytes 221192 | tf_op jit(solution)/shard_map/ppermute | solution.py:319
  371.6 23.7 %all-to-all-start.7 = ((bf16[8,128,256]{2,1,0:T(8,128)(2,1)}), bf16[8,128,256]{2,1,0:T(8,128)(2,1)S(1)}, u32[]{:S(2)}, u32[]{:S(2)}) async-start(bf16[8,128,256]{2,1,0:T(8,128)(2,1)} %shard_map.99), calls=%async_computation.7 | async-start | bytes 1048576 | tf_op jit(solution)/shard_map/all_to_all | solution.py:417
  397.9 11.9 %collective-permute-start.19 = (bf16[144,256]{1,0:T(8,128)(2,1)}, bf16[144,256]{1,0:T(8,128)(2,1)S(1)}, u32[]{:S(2)}, u32[]{:S(2)}) collective-permute-start(bf16[144,256]{1,0:T(8,128)(2,1)} %get-tuple-element.141.send_ref), channel_id=1, source_target_pairs={{2,0},{4,2},{6,4},{8,6},{10,8},{12,10},{14,12},{16,14},{18,16},{20... | collective-permute-start | bytes 221192 | tf_op jit(solution)/shard_map/ppermute | solution.py:319
  423.4 23.7 %all-to-all-start.8 = ((bf16[8,128,256]{2,1,0:T(8,128)(2,1)}), bf16[8,128,256]{2,1,0:T(8,128)(2,1)S(1)}, u32[]{:S(2)}, u32[]{:S(2)}) async-start(bf16[8,128,256]{2,1,0:T(8,128)(2,1)} %shard_map.103), calls=%async_computation.8 | async-start | bytes 1048576 | tf_op jit(solution)/shard_map/all_to_all | solution.py:417
  449.7 12.0 %collective-permute-start.22 = (bf16[144,256]{1,0:T(8,128)(2,1)}, bf16[144,256]{1,0:T(8,128)(2,1)S(1)}, u32[]{:S(2)}, u32[]{:S(2)}) collective-permute-start(bf16[144,256]{1,0:T(8,128)(2,1)} %get-tuple-element.150.send_ref), channel_id=1, source_target_pairs={{2,0},{4,2},{6,4},{8,6},{10,8},{12,10},{14,12},{16,14},{18,16},{20... | collective-permute-start | bytes 221192 | tf_op jit(solution)/shard_map/ppermute | solution.py:319
  475.2 23.7 %all-to-all-start.9 = ((bf16[8,128,256]{2,1,0:T(8,128)(2,1)}), bf16[8,128,256]{2,1,0:T(8,128)(2,1)S(1)}, u32[]{:S(2)}, u32[]{:S(2)}) async-start(bf16[8,128,256]{2,1,0:T(8,128)(2,1)} %shard_map.107), calls=%async_computation.9 | async-start | bytes 1048576 | tf_op jit(solution)/shard_map/all_to_all | solution.py:417
  501.5 28.7 %collective-permute-start.25 = (bf16[144,256]{1,0:T(8,128)(2,1)}, bf16[144,256]{1,0:T(8,128)(2,1)S(1)}, u32[]{:S(2)}, u32[]{:S(2)}) collective-permute-start(bf16[144,256]{1,0:T(8,128)(2,1)} %get-tuple-element.159.send_ref), channel_id=1, source_target_pairs={{2,0},{4,2},{6,4},{8,6},{10,8},{12,10},{14,12},{16,14},{18,16},{20... | collective-permute-start | bytes 221192 | tf_op jit(solution)/shard_map/ppermute | solution.py:319
  506.1 24.1 %collective-permute-start.26 = (bf16[16,256]{1,0:T(8,128)(2,1)}, bf16[16,256]{1,0:T(8,128)(2,1)S(1)}, u32[]{:S(2)}, u32[]{:S(2)}) collective-permute-start(bf16[16,256]{1,0:T(8,128)(2,1)} %get-tuple-element.161), channel_id=1, source_target_pairs={{4,0},{6,2},{8,4},{10,6},{12,8},{14,10},{16,12},{18,14},{20,16},{2... | collective-permute-start | bytes 24584 | tf_op jit(solution)/shard_map/ppermute | solution.py:319
  (59 other events, 275.1 us)
Sparse Core Ops, SparseCore 0:
  54.4 54.4 all-gather.8
  111.3 46.7 all-gather.10
  160.6 49.3 all-gather.12
  212.2 49.4 all-gather.14
  264.1 49.1 all-gather.16
  315.6 49.3 all-gather.18
  367.4 49.3 all-gather.20
  419.2 49.3 all-gather.22
